TPU v7x, 32 devices: a whole 2x2x4 slice. The times are simulated.
32 devices in a mesh: groups: 2 (over y), row: 8 (over z, x), section: 2 (over core).
Axes of the slice: x: 2, y: 2, z: 4, core: 2. Of those that a mesh axis runs over, the one named last changes fastest.
Arguments:
- hidden: bfloat16 [64, 8192], P('groups', ('row', 'section')), parts along dimension 0, may hold values from -6 to 6
- norm_in_gain: float32 [8192], replicated, may hold values from 0.1 to 1.9
- zx_weight: bfloat16 [8192, 2, 8, 64], P(None, None, 'row', 'section'), may hold values from -0.0625 to 0.0625
- bc_weight: bfloat16 [8192, 2048], P(None, ('row', 'section')), may hold values from -0.0625 to 0.0625
- dt_weight: bfloat16 [8192, 8], P(None, 'row'), may hold values from -0.0625 to 0.0625
- dt_bias: float32 [8], P('row'), may hold values from -3 to -0.5
- decay_log: float32 [8], P('row'), may hold values from -0.7 to 2
- skip_gain: float32 [8], P('row'), may hold values from 0.5 to 1.5
- conv_x_weight: float32 [4, 8, 64], P(None, 'row', 'section'), may hold values from -3.6 to 3.6
- conv_x_bias: float32 [8, 64], P('row', 'section'), may hold values from -3 to 3
- conv_bc_weight: float32 [4, 2048], P(None, ('row', 'section')), may hold values from -3 to 3
- conv_bc_bias: float32 [2048], P(('row', 'section')), may hold values from -3 to 3
- conv_x_state: bfloat16 [64, 3, 8, 64], P('groups', None, 'row', 'section'), parts along dimension 0, may hold values from -6 to 6
- conv_bc_state: bfloat16 [64, 3, 2048], P('groups', None, ('row', 'section')), parts along dimension 0, may hold values from -6 to 6
- ssm_state: bfloat16 [64, 8, 64, 256], P('groups', 'row', 'section'), parts along dimension 0, may hold values from -6 to 6
- gate_norm_weight: float32 [8, 64], P('row', 'section'), may hold values from 0.1 to 1.9
- out_weight: bfloat16 [8, 64, 8192], P('row', 'section'), may hold values from -0.375 to 0.375
- norm_mid_gain: float32 [8192], replicated, may hold values from 0.1 to 1.9
- up_weight: bfloat16 [8192, 16384], P(None, ('row', 'section')), may hold values from -0.0625 to 0.0625
- down_weight: bfloat16 [16384, 8192], P(('row', 'section')), may hold values from -0.0625 to 0.0625
- valid: int32 [64], P('groups'), parts along dimension 0, may hold values 0 or 1
Outputs:
- block_out: bfloat16 [64, 8192], P('groups', ('row', 'section')), parts along dimension 0
- new_ssm_state: bfloat16 [64, 8, 64, 256], P('groups', 'row', 'section'), parts along dimension 0
- new_conv_x_state: bfloat16 [64, 3, 8, 64], P('groups', None, 'row', 'section'), parts along dimension 0
- new_conv_bc_state: bfloat16 [64, 3, 2048], P('groups', None, ('row', 'section')), parts along dimension 0
There are 2 independent parts, one for each index of `groups`. A program takes and returns all parts, laid end to end along the dimension named above; an argument that names none is the same for every part. Nothing has to cross between parts.
All inputs are finite; a program needn't handle non-finite values.
Results may differ from a plain program's by a relative error of at most 0.0075.
Values may be sent and summed in bfloat16 or wider, within the bound.
A program may use at most 128 MiB of HBM per device.

v0:
```python
import jax
import jax.numpy as jnp
from jax import lax
from jax.sharding import PartitionSpec as P

D = 8192
HEAD_DIM = 64
STATE = 256
GROUPS = 4


def mean_norm(values, gain):
    return values * lax.rsqrt(jnp.mean(values * values, axis=-1, keepdims=True) + 1e-05) * gain


def body(
    hidden,
    norm_in_gain,
    zx_weight,
    bc_weight,
    dt_weight,
    dt_bias,
    decay_log,
    skip_gain,
    conv_x_weight,
    conv_x_bias,
    conv_bc_weight,
    conv_bc_bias,
    conv_x_state,
    conv_bc_state,
    ssm_state,
    gate_norm_weight,
    out_weight,
    norm_mid_gain,
    up_weight,
    down_weight,
    valid,
):
    row_count = hidden.shape[0]
    local_p = zx_weight.shape[3]
    full_rows = lax.all_gather(hidden, ("row", "section"), axis=1, tiled=True)
    normed = mean_norm(full_rows.astype(jnp.float32), norm_in_gain).astype(jnp.bfloat16)
    gate_inner = jnp.dot(
        normed, zx_weight.reshape(D, 2 * local_p), preferred_element_type=jnp.float32
    ).reshape(row_count, 2, 1, local_p)
    gate_part = gate_inner[:, 0]
    inner_pre = gate_inner[:, 1].astype(jnp.bfloat16)
    bc_pre = jnp.dot(normed, bc_weight, preferred_element_type=jnp.float32).astype(jnp.bfloat16)
    dt_raw = jnp.dot(normed, dt_weight, preferred_element_type=jnp.float32)
    taps_x = jnp.concatenate([conv_x_state, inner_pre[:, None]], axis=1)
    inner = jax.nn.silu(
        jnp.sum(taps_x.astype(jnp.float32) * conv_x_weight[None], axis=1) + conv_x_bias
    )
    taps_bc = jnp.concatenate([conv_bc_state, bc_pre[:, None]], axis=1)
    mixed_bc = jax.nn.silu(
        jnp.sum(taps_bc.astype(jnp.float32) * conv_bc_weight[None], axis=1) + conv_bc_bias
    )
    all_bc = lax.all_gather(mixed_bc, ("row", "section"), axis=1, tiled=True)
    per_group = lax.axis_size("row") // GROUPS
    group_index = lax.axis_index("row") // per_group
    state_in = all_bc[:, : GROUPS * STATE].reshape(row_count, GROUPS, STATE)
    state_out = all_bc[:, GROUPS * STATE :].reshape(row_count, GROUPS, STATE)
    in_mine = lax.dynamic_slice_in_dim(state_in, group_index, 1, axis=1)
    out_mine = lax.dynamic_slice_in_dim(state_out, group_index, 1, axis=1)
    step_size = jax.nn.softplus(dt_raw + dt_bias[None])
    decay_rate = jnp.exp(-step_size * jnp.exp(decay_log)[None])
    previous = ssm_state.astype(jnp.float32)
    updated = (
        decay_rate[:, :, None, None] * previous
        + (step_size[:, :, None] * inner)[..., None] * in_mine[:, :, None, :]
    )
    readout = (
        jnp.einsum("rhpn,rhn->rhp", updated, out_mine, precision=lax.Precision.HIGHEST)
        + skip_gain[None, :, None] * inner
    )
    gated = readout * jax.nn.silu(gate_part)
    local_squares = jnp.sum(gated * gated, axis=(1, 2))
    group_pick = (jnp.arange(GROUPS) == group_index).astype(jnp.float32)
    group_sums = lax.psum(local_squares[:, None] * group_pick[None], ("row", "section"))
    group_size = per_group * HEAD_DIM
    group_mean = jnp.sum(group_sums * group_pick[None], axis=1) / group_size
    scaled = (gated * lax.rsqrt(group_mean + 1e-05)[:, None, None] * gate_norm_weight[None]).astype(
        jnp.bfloat16
    )
    mixer_terms = jnp.dot(
        scaled.reshape(row_count, local_p),
        out_weight.reshape(local_p, D),
        preferred_element_type=jnp.float32,
    )
    mixer_share = lax.psum_scatter(mixer_terms, ("row", "section"), scatter_dimension=1, tiled=True)
    middle = (hidden.astype(jnp.float32) + mixer_share).astype(jnp.bfloat16)
    middle_full = lax.all_gather(middle, ("row", "section"), axis=1, tiled=True)
    mlp_in = mean_norm(middle_full.astype(jnp.float32), norm_mid_gain).astype(jnp.bfloat16)
    up_values = jnp.dot(mlp_in, up_weight, preferred_element_type=jnp.float32)
    activated = jnp.square(jax.nn.relu(up_values)).astype(jnp.bfloat16)
    down_terms = jnp.dot(activated, down_weight, preferred_element_type=jnp.float32)
    down_share = lax.psum_scatter(down_terms, ("row", "section"), scatter_dimension=1, tiled=True)
    block_out = (middle.astype(jnp.float32) + down_share).astype(jnp.bfloat16)
    kept_rows = valid != 0
    new_ssm_state = jnp.where(kept_rows[:, None, None, None], updated, previous).astype(
        jnp.bfloat16
    )
    new_conv_x_state = jnp.where(kept_rows[:, None, None, None], taps_x[:, 1:], conv_x_state)
    new_conv_bc_state = jnp.where(kept_rows[:, None, None], taps_bc[:, 1:], conv_bc_state)
    return (block_out, new_ssm_state, new_conv_x_state, new_conv_bc_state)


def solution(mesh):
    return jax.shard_map(
        body,
        mesh=mesh,
        in_specs=(
            P("groups", ("row", "section")),
            P(),
            P(None, None, "row", "section"),
            P(None, ("row", "section")),
            P(None, "row"),
            P("row"),
            P("row"),
            P("row"),
            P(None, "row", "section"),
            P("row", "section"),
            P(None, ("row", "section")),
            P(("row", "section")),
            P("groups", None, "row", "section"),
            P("groups", None, ("row", "section")),
            P("groups", "row", "section", None),
            P("row", "section"),
            P("row", "section", None),
            P(),
            P(None, ("row", "section")),
            P(("row", "section"), None),
            P("groups"),
        ),
        out_specs=(
            P("groups", ("row", "section")),
            P("groups", "row", "section", None),
            P("groups", None, "row", "section"),
            P("groups", None, ("row", "section")),
        ),
        check_vma=False,
    )
```

profile of v0, /device:TPU:0, one launch (start us, length us, event | category | flops | bytes accessed | tf_op | source)
XLA Modules:
  0.0 251.6 jit_solution(10273601416538449090)
XLA Ops:
  7.3 24.9 %all_gather.9 = bf16[32,8192]{1,0:T(8,128)(2,1)S(1)} all-gather(bf16[32,512]{1,0:T(8,128)(2,1)} %param.21), channel_id=1, replica_groups=mesh['groups'=2,'row'=8,'section'=2] {'row','section'}, dimensions={1}, use_global_device_ids=true | all-gather | bytes 557056 | tf_op jit(solution)/shard_map/all_gather | solution.py:41
  32.2 0.2 fusion.4
  32.4 1.7 convolution_bitcast_fusion
  34.3 0.8 multiply_reduce_fusion.1
  35.8 1.2 fusion.2
  37.0 0.8 multiply_reduce_fusion
  37.8 0.7 divide_multiply_fusion
  38.4 18.1 %all_gather.10 = f32[32,2048]{1,0:T(8,128)S(1)} all-gather(f32[32,128]{1,0:T(8,128)S(1)} %divide_multiply_fusion), channel_id=1, replica_groups=mesh['groups'=2,'row'=8,'section'=2] {'row','section'}, dimensions={1}, use_global_device_ids=true | all-gather | bytes 278528 | tf_op jit(solution)/shard_map/all_gather | solution.py:58
  58.1 1.1 multiply_exponential_fusion
  59.2 0.8 broadcast_multiply_fusion
  60.1 2.3 fusion.13
  62.4 0.8 multiply_reduce_fusion.2
  63.3 31.1 %psum.7 = f32[32,4]{0,1:T(4,128)S(1)} all-reduce(f32[32,4]{0,1:T(4,128)S(1)} %broadcast_multiply_fusion.1), channel_id=1, replica_groups=mesh['groups'=2,'row'=8,'section'=2] {'row','section'}, use_global_device_ids=true, to_apply=%region_4.5 | all-reduce | flops 128 | bytes 1024 | tf_op jit(solution)/shard_map/psum | solution.py:79
  94.5 2.5 fusion.19
  97.0 54.8 %reduce-scatter.3.cloned.1.call-done = f32[32,512]{1,0:T(8,128)} async-done(((f32[32,8192]{1,0:T(8,128)}), f32[32,512]{1,0:T(8,128)}) %reduce-scatter.3.cloned.1.call-update) | async-done | bytes 65552 | tf_op jit(solution)/shard_map/reduce_scatter | solution.py:90
  151.8 0.8 add_convert_fusion.1
  152.6 20.8 %all_gather.11 = bf16[32,8192]{1,0:T(8,128)(2,1)S(1)} all-gather(bf16[32,512]{1,0:T(8,128)(2,1)S(1)} %add_convert_fusion.1), channel_id=1, replica_groups=mesh['groups'=2,'row'=8,'section'=2] {'row','section'}, dimensions={1}, use_global_device_ids=true | all-gather | bytes 557056 | tf_op jit(solution)/shard_map/all_gather | solution.py:92
  173.5 0.2 fusion.9
  173.7 14.8 %fusion.16 = f32[32,8192]{1,0:T(8,128)} fusion(bf16[1024,8192]{1,0:T(8,128)(2,1)} %param.40, bf16[8192,1024]{1,0:T(8,128)(2,1)} %param.39, bf16[32,8192]{1,0:T(8,128)(2,1)S(1)} %all_gather.11, f32[8192]{0:T(1024)} %param.38, f32[32]{0:T(128)S(1)} %add_rsqrt_fusion), kind=kOutput, calls=%fused_computation.25 | convolution fusion | flops 1074888704 | bytes 35160192 | tf_op jit(solution)/shard_map/dot_general | solution.py:96
  188.6 0.7 fusion.35
  189.2 0.7 fusion.33
  189.9 1.2 fusion.8
  191.1 52.2 %reduce-scatter.5.cloned.1.call-done = f32[32,512]{1,0:T(8,128)} async-done(((f32[32,8192]{1,0:T(8,128)}), f32[32,512]{1,0:T(8,128)}) %reduce-scatter.5.cloned.1.call-update) | async-done | bytes 65552 | tf_op jit(solution)/shard_map/reduce_scatter | solution.py:97
  243.3 1.5 add_convert_fusion
  (31 shorter events, 0.8 us)
Async XLA Ops:
  7.2 28.6 %copy-start = (bf16[8192,128]{1,0:T(8,128)(2,1)S(1)}, bf16[8192,128]{1,0:T(8,128)(2,1)}, u32[]{:S(2)}) copy-start(bf16[8192,128]{1,0:T(8,128)(2,1)} %param.24) | copy-start | bytes 6291460
  7.2 144.6 %reduce-scatter.3.cloned.1.call-start = ((), (), s32[]{:S(2)}) async-start(), calls=%async_computation.2 | async-start | bytes 1114112 | tf_op jit(solution)/shard_map/reduce_scatter | solution.py:90
  96.9 146.4 %reduce-scatter.5.cloned.1.call-start = ((), (), s32[]{:S(2)}) async-start(), calls=%async_computation.3 | async-start | bytes 1114112 | tf_op jit(solution)/shard_map/reduce_scatter | solution.py:97
  173.7 14.8 %copy-start.4 = (s32[32]{0:T(128)S(1)}, s32[32]{0:T(128)}, u32[]{:S(2)}) copy-start(s32[32]{0:T(128)} %param.41) | copy-start | bytes 388
  173.7 14.8 %copy-start.2 = (bf16[32,3,1,32]{3,0,2,1:T(8,128)(2,1)S(1)}, bf16[32,3,1,32]{3,0,2,1:T(8,128)(2,1)}, u32[]{:S(2)}) copy-start(bf16[32,3,1,32]{3,0,2,1:T(8,128)(2,1)} %param.33) | copy-start | bytes 18436
  173.7 15.5 %copy-start.3 = (bf16[32,3,128]{2,0,1:T(8,128)(2,1)S(1)}, bf16[32,3,128]{2,0,1:T(8,128)(2,1)}, u32[]{:S(2)}) copy-start(bf16[32,3,128]{2,0,1:T(8,128)(2,1)} %param.34) | copy-start | bytes 73732
  173.7 16.2 %copy-start.1 = (bf16[32,1,32,256]{3,2,1,0:T(8,128)(2,1)S(1)}, bf16[32,1,32,256]{3,2,1,0:T(8,128)(2,1)}, u32[]{:S(2)}) copy-start(bf16[32,1,32,256]{3,2,1,0:T(8,128)(2,1)} %param.35) | copy-start | bytes 1572868
Sparse Core Ops, SparseCore 0:
  97.1 54.6 reduce-scatter.2
  188.6 54.6 reduce-scatter.4
where the time goes:
time: 252 us
  waiting for transfers between devices  107 us (42%)
  blocking collectives  95 us (38%)
  matrix products  23.5 us (9%)
  between operations  16.2 us (6%)
  other arithmetic  9.25 us (4%)
    reduce_scatter x1, waiting for transfers between devices, body(): lax.psum_scatter(mixer_terms, ('row', 'section'), scatter_dimension=1, ti...  54.8 us
    reduce_scatter x1, waiting for transfers between devices, body(): lax.psum_scatter(down_terms, ('row', 'section'), scatter_dimension=1, til...  52.2 us
    psum x1, blocking collectives, body(): lax.psum(local_squares[:, None] * group_pick[None], ('row', 'section'))  31.1 us
    all_gather x1, blocking collectives, body(): full_rows = lax.all_gather(hidden, ('row', 'section'), axis=1, tiled=True)  24.9 us
    all_gather x1, blocking collectives, body(): middle_full = lax.all_gather(middle, ('row', 'section'), axis=1, tiled=True)  20.8 us
    all_gather x1, blocking collectives, body(): all_bc = lax.all_gather(mixed_bc, ('row', 'section'), axis=1, tiled=True)  18.1 us
    dot_general x1, matrix products, body(): jnp.dot(activated, down_weight, preferred_element_type=jnp.float32)  14.8 us
  transfers between devices with their start and end apart: 2, of which 2 were waited for; matrix products, arithmetic and copies ran while one was open for 1% of the time, Pallas kernels for 0%

commit v1 on v0

--- a/solution.py
+++ b/solution.py
@@ -1,6 +1,10 @@
+import functools
+
 import jax
 import jax.numpy as jnp
 from jax import lax
+from jax.experimental import pallas as pl
+from jax.experimental.pallas import tpu as pltpu
 from jax.sharding import PartitionSpec as P
 
 D = 8192
@@ -105,9 +109,418 @@
     return (block_out, new_ssm_state, new_conv_x_state, new_conv_bc_state)
 
 
+HI = lax.Precision.HIGHEST
+MESH = pl.DeviceIdType.MESH
+NT = (((1,), (1,)), ((), ()))
+
+
+def fits(mesh):
+    rows, sections = mesh.shape["row"], mesh.shape["section"]
+    devices = rows * sections
+    return sections == 2 and devices == 16 and rows % GROUPS == 0
+
+
+def silu(values):
+    return values / (1.0 + jnp.exp(-values))
+
+
+def fused_kernel(
+    R,
+    hid, gin, zxt, bcw, dtt, dtb, dlog, skip, cxw, cxb, cbw, cbb, cxs, cbs, ssm, gnw, outw, gmid,
+    upw, dnw, valid,
+    out, new_ssm, new_cx, new_cb,
+    zx_v, bc_v, ssm_v, up_v, dn_v, hid_all, owt, bc_out, bc_all, g_out, g_all, mid, mid_all,
+    act, send_a, recv_a, send_b, recv_b, own_sum,
+    w_sem, h_send, h_recv, o_send, o_recv, bc_send, bc_recv, g_send, g_recv, m_send, m_recv,
+    a_send, a_recv, b_send, b_recv,
+):
+    N = 2 * R
+    grp, row, sec = lax.axis_index("groups"), lax.axis_index("row"), lax.axis_index("section")
+    me = row * 2 + sec
+    other = 1 - sec
+    rows, wd = hid.shape
+    local_p = zxt.shape[0] // 2
+    model = upw.shape[0]
+
+    def remote(src, dst, ssem, rsem, r, s):
+        return pltpu.make_async_remote_copy(
+            src_ref=src, dst_ref=dst, send_sem=ssem, recv_sem=rsem,
+            device_id=(grp, r, s), device_id_type=MESH,
+        )
+
+    pending = []
+
+    loads = [
+        pltpu.make_async_copy(bcw, bc_v, w_sem.at[0]),
+        pltpu.make_async_copy(zxt, zx_v, w_sem.at[1]),
+        pltpu.make_async_copy(ssm, ssm_v, w_sem.at[2]),
+        pltpu.make_async_copy(upw, up_v, w_sem.at[3]),
+        pltpu.make_async_copy(dnw, dn_v, w_sem.at[4]),
+    ]
+
+    barrier = pltpu.get_barrier_semaphore()
+    for k in range(1, N):
+        peer = lax.rem(me + k, N)
+        pl.semaphore_signal(
+            barrier, inc=1, device_id=(grp, peer // 2, peer % 2), device_id_type=MESH
+        )
+    for copy in loads:
+        copy.start()
+    hid_all[me] = hid[...]
+    pl.semaphore_wait(barrier, N - 1)
+
+    def gather_start(src, buf, ssem, rsem):
+        for k in range(1, R):
+            copy = remote(src, buf.at[me], ssem.at[k], rsem.at[me], lax.rem(row + k, R), sec)
+            copy.start()
+            pending.append(copy)
+        copy = remote(src, buf.at[me], ssem.at[0], rsem.at[me], row, other)
+        copy.start()
+        pending.append(copy)
+
+    def gather_finish(buf, ssem, rsem):
+        for k in range(1, R):
+            blk = lax.rem(row + R - k, R) * 2 + sec
+            copy = remote(buf.at[blk], buf.at[blk], ssem.at[R + k - 1], rsem.at[blk], row, other)
+            copy.wait_recv()
+            copy.start()
+            pending.append(copy)
+        for k in range(R):
+            blk = lax.rem(row + R - k, R) * 2 + other
+            remote(buf.at[blk], buf.at[blk], ssem.at[0], rsem.at[blk], row, other).wait_recv()
+
+    gather_start(hid, hid_all, h_send, h_recv)
+
+    eye = (
+        lax.broadcasted_iota(jnp.int32, (local_p, local_p), 0)
+        == lax.broadcasted_iota(jnp.int32, (local_p, local_p), 1)
+    ).astype(jnp.float32)
+
+    def turn(values):
+        return lax.dot_general(eye, values, NT, precision=HI, preferred_element_type=jnp.float32)
+
+    f32 = jnp.float32
+    valid_row = (valid[...] != 0).astype(f32)
+    valid_col = turn(valid_row)
+    pre_x = cxb[...] + sum(cxs[t].astype(f32) * cxw[t : t + 1, :] for t in range(3))
+    pre_x_t = turn(pre_x)
+    tap_t = turn(cxw[3:4, :])
+    gnw_t = turn(gnw[...])
+    pre_bc = cbb[...] + sum(cbs[t].astype(f32) * cbw[t : t + 1, :] for t in range(3))
+
+    gather_finish(hid_all, h_send, h_recv)
+
+    for k in range(1, N):
+        peer = lax.rem(me + k, N)
+        copy = remote(
+            outw.at[:, pl.ds(pl.multiple_of(peer * wd, wd), wd)],
+            owt.at[me], o_send.at[k], o_recv.at[me], peer // 2, peer % 2,
+        )
+        copy.start()
+        pending.append(copy)
+    own_w = pltpu.make_async_copy(
+        outw.at[:, pl.ds(pl.multiple_of(me * wd, wd), wd)], owt.at[me], w_sem.at[5]
+    )
+    own_w.start()
+
+    def inverse_norm(buf):
+        def step(b, total):
+            values = buf[b].astype(f32)
+            squares = values * values
+            return total + sum(squares[:, i : i + 128] for i in range(0, wd, 128))
+
+        total = lax.fori_loop(0, N, step, jnp.zeros((rows, 128), f32))
+        return lax.rsqrt(jnp.sum(total, axis=1, keepdims=True) / model + 1e-05)
+
+    scale = inverse_norm(hid_all)
+    loads[0].wait()
+    loads[1].wait()
+
+    def project(b, carry):
+        acc_bc, acc_zx, acc_dt = carry
+        at = pl.ds(pl.multiple_of(b * wd, wd), wd)
+        normed = (hid_all[b].astype(f32) * scale * gin[:, at]).astype(jnp.bfloat16)
+        acc_bc += jnp.dot(normed, bc_v[at, :], preferred_element_type=f32)
+        acc_zx += lax.dot_general(zx_v[:, at], normed, NT, preferred_element_type=f32)
+        dt_rows = jnp.broadcast_to(dtt[:, at].astype(f32), (16, wd)).astype(jnp.bfloat16)
+        acc_dt += lax.dot_general(dt_rows, normed, NT, preferred_element_type=f32)
+        return acc_bc, acc_zx, acc_dt
+
+    acc_bc, acc_zx, acc_dt = lax.fori_loop(
+        0, N, project,
+        (
+            jnp.zeros((rows, bc_v.shape[1]), f32),
+            jnp.zeros((2 * local_p, rows), f32),
+            jnp.zeros((16, rows), f32),
+        ),
+    )
+    bc_pre = acc_bc.astype(jnp.bfloat16).astype(f32)
+    mixed_bc = silu(pre_bc + bc_pre * cbw[3:4, :])
+    bc_out[...] = mixed_bc
+
+    cb = bc_v.shape[1]
+    parts = STATE // cb
+    half = me // (N // 2)
+    to_group = lax.rem(me, N // 2) // parts
+    slot = half * parts + lax.rem(me, parts)
+    per = N // GROUPS
+    my_group = me // per
+    for i in range(per):
+        dest = to_group * per + i
+
+        @pl.when(dest != me)
+        def _():
+            remote(
+                bc_out, bc_all.at[slot], bc_send.at[i], bc_recv.at[slot], dest // 2, dest % 2
+            ).start()
+
+        @pl.when(dest == me)
+        def _():
+            bc_all[slot] = bc_out[...]
+
+    gate_t = silu(acc_zx[:local_p])
+    inner_pre_t = acc_zx[local_p:].astype(jnp.bfloat16).astype(f32)
+    inner_t = silu(pre_x_t + inner_pre_t * tap_t)
+    dt_sum = acc_dt[0:1] + dtb[...]
+    step_size = jnp.maximum(dt_sum, 0.0) + jnp.log1p(jnp.exp(-jnp.abs(dt_sum)))
+    decay = jnp.exp(-step_size * jnp.exp(dlog[...]))
+    driven_t = inner_t * step_size
+    keep_x = jnp.broadcast_to(valid_col, (rows, local_p)) > 0.5
+    keep_bc = jnp.broadcast_to(valid_col, (rows, cb)) > 0.5
+    last_x = turn(inner_pre_t)
+    for t in range(3):
+        later_x = last_x if t == 2 else cxs[t + 1].astype(f32)
+        later_bc = bc_pre if t == 2 else cbs[t + 1].astype(f32)
+        new_cx[t] = jnp.where(keep_x, later_x, cxs[t].astype(f32)).astype(jnp.bfloat16)
+        new_cb[t] = jnp.where(keep_bc, later_bc, cbs[t].astype(f32)).astype(jnp.bfloat16)
+    loads[2].wait()
+
+    for h in range(2):
+        for p in range(parts):
+            source = h * (N // 2) + my_group * parts + p
+
+            @pl.when(source != me)
+            def _():
+                remote(
+                    bc_out, bc_all.at[h * parts + p], bc_send.at[0], bc_recv.at[h * parts + p],
+                    row, other,
+                ).wait_recv()
+
+    state_in = jnp.concatenate([bc_all[p] for p in range(parts)], axis=1)
+    state_out = jnp.concatenate([bc_all[parts + p] for p in range(parts)], axis=1)
+
+    lane = lax.broadcasted_iota(jnp.int32, (local_p, rows), 1)
+
+    def updated(r):
+        previous = ssm_v[r].astype(f32)
+        value = decay[0:1, r : r + 1] * previous + driven_t[:, r : r + 1] * state_in[r : r + 1, :]
+        return previous, value
+
+    read_t = jnp.zeros((local_p, rows), f32)
+    for r in range(rows):
+        _, value = updated(r)
+        column = jnp.sum(value * state_out[r : r + 1, :], axis=1, keepdims=True)
+        read_t = jnp.where(lane == r, column, read_t)
+    gated_t = (read_t + skip[...] * inner_t) * gate_t
+    g_out[:, 0:rows] = gated_t
+    g_out[:, rows : rows + 1] = gnw_t
+    gather_start(g_out, g_all, g_send, g_recv)
+    g_all[me] = g_out[...]
+
+    for r in range(rows):
+        previous, value = updated(r)
+        keep = jnp.broadcast_to(valid_row[0:1, r : r + 1], value.shape) > 0.5
+        new_ssm[r] = jnp.where(keep, value, previous).astype(jnp.bfloat16)
+
+    for k in range(1, N):
+        peer = lax.rem(me + N - k, N)
+        remote(owt.at[peer], owt.at[peer], o_send.at[0], o_recv.at[peer], row, other).wait_recv()
+    own_w.wait()
+    gather_finish(g_all, g_send, g_recv)
+
+    eye_rows = (
+        lax.broadcasted_iota(jnp.int32, (rows, rows), 0)
+        == lax.broadcasted_iota(jnp.int32, (rows, rows), 1)
+    ).astype(jnp.bfloat16)
+    mixed = hid[...].astype(f32)
+    for q in range(GROUPS):
+        pieces = [g_all[q * per + i, :, 0:rows] for i in range(per)]
+        squares = sum(jnp.sum(piece * piece, axis=0, keepdims=True) for piece in pieces)
+        norm = lax.rsqrt(squares / (per * local_p) + 1e-05)
+        scaled_t = jnp.concatenate(
+            [pieces[i] * norm * g_all[q * per + i, :, rows : rows + 1] for i in range(per)], axis=0
+        ).astype(jnp.bfloat16)
+        scaled = lax.dot_general(eye_rows, scaled_t, NT, preferred_element_type=f32)
+        weights = owt[q * per : (q + 1) * per].reshape(per * local_p, wd)
+        mixed += jnp.dot(scaled.astype(jnp.bfloat16), weights, preferred_element_type=f32)
+    mid[...] = mixed.astype(jnp.bfloat16)
+    gather_start(mid, mid_all, m_send, m_recv)
+    mid_all[me] = mid[...]
+    gather_finish(mid_all, m_send, m_recv)
+
+    scale_mid = inverse_norm(mid_all)
+    loads[3].wait()
+    ff = up_v.shape[1]
+    act[...] = jnp.zeros_like(act)
+
+    def up_step(b, _):
+        at = pl.ds(pl.multiple_of(b * wd, wd), wd)
+        fed = (mid_all[b].astype(f32) * scale_mid * gmid[:, at]).astype(jnp.bfloat16)
+        act[...] += jnp.dot(fed, up_v[at, :], preferred_element_type=f32)
+        return 0
+
+    lax.fori_loop(0, N, up_step, 0)
+    activated = jnp.square(jnp.maximum(act[...], 0.0)).astype(jnp.bfloat16)
+    loads[4].wait()
+
+    def down(block):
+        at = pl.ds(pl.multiple_of(block * wd, wd), wd)
+        return jnp.dot(activated, dn_v[:, at], preferred_element_type=f32)
+
+    def for_partner(k, _):
+        target = lax.rem(row + 1 + k, R)
+        send_a[k] = down(target * 2 + other).astype(jnp.bfloat16)
+        remote(send_a.at[k], recv_a.at[k], a_send.at[k], a_recv.at[k], row, other).start()
+        return 0
+
+    lax.fori_loop(0, R, for_partner, 0)
+
+    def for_chip(k, _):
+        target = lax.rem(row + 1 + k, R)
+        part = down(target * 2 + sec)
+        remote(send_a.at[k], recv_a.at[k], a_send.at[k], a_recv.at[k], row, other).wait()
+        send_b[k] = (part + recv_a[k].astype(f32)).astype(jnp.bfloat16)
+        remote(send_b.at[k], recv_b.at[row], b_send.at[k], b_recv.at[row], target, sec).start()
+        return 0
+
+    lax.fori_loop(0, R - 1, for_chip, 0)
+    total = down(me)
+    remote(
+        send_a.at[R - 1], recv_a.at[R - 1], a_send.at[R - 1], a_recv.at[R - 1], row, other
+    ).wait()
+    own_sum[...] = total + recv_a[R - 1].astype(f32) + mid[...].astype(f32)
+
+    def collect(k, _):
+        source = lax.rem(row + R - 1 - k, R)
+        remote(
+            send_b.at[k], recv_b.at[source], b_send.at[k], b_recv.at[source], source, sec
+        ).wait_recv()
+        own_sum[...] += recv_b[source].astype(f32)
+        return 0
+
+    lax.fori_loop(0, R - 1, collect, 0)
+    out[...] = own_sum[...].astype(jnp.bfloat16)
+
+    def drain(k, _):
+        remote(
+            send_b.at[k], recv_b.at[row], b_send.at[k], b_recv.at[row], row, other
+        ).wait_send()
+        return 0
+
+    lax.fori_loop(0, R - 1, drain, 0)
+    for i in range(per):
+        dest = to_group * per + i
+
+        @pl.when(dest != me)
+        def _():
+            remote(
+                bc_out, bc_all.at[slot], bc_send.at[i], bc_recv.at[slot], row, other
+            ).wait_send()
+
+    for copy in pending:
+        copy.wait_send()
+
+
+def fused_body(
+    hidden, norm_in_gain, zx_weight, bc_weight, dt_weight, dt_bias, decay_log, skip_gain,
+    conv_x_weight, conv_x_bias, conv_bc_weight, conv_bc_bias, conv_x_state, conv_bc_state,
+    ssm_state, gate_norm_weight, out_weight, norm_mid_gain, up_weight, down_weight, valid,
+):
+    R = lax.axis_size("row")
+    N = 2 * R
+    rows, wd = hidden.shape
+    model = up_weight.shape[0]
+    p = zx_weight.shape[3]
+    cb = bc_weight.shape[1]
+    ff = up_weight.shape[1]
+    bf16, f32 = jnp.bfloat16, jnp.float32
+    vm, hbm = pl.BlockSpec(memory_space=pltpu.VMEM), pl.BlockSpec(memory_space=pl.ANY)
+    dma = pltpu.SemaphoreType.DMA
+    out, new_ssm, new_cx, new_cb = pl.pallas_call(
+        functools.partial(fused_kernel, R),
+        out_shape=(
+            jax.ShapeDtypeStruct((rows, wd), bf16),
+            jax.ShapeDtypeStruct((rows, p, STATE), bf16),
+            jax.ShapeDtypeStruct((3, rows, p), bf16),
+            jax.ShapeDtypeStruct((3, rows, cb), bf16),
+        ),
+        in_specs=[
+            vm, vm, hbm, hbm, vm, vm, vm, vm, vm, vm, vm, vm, vm, vm, hbm, vm, hbm, vm, hbm, hbm, vm
+        ],
+        out_specs=(vm, vm, vm, vm),
+        scratch_shapes=[
+            pltpu.VMEM((2 * p, model), bf16),
+            pltpu.VMEM((model, cb), bf16),
+            pltpu.VMEM((rows, p, STATE), bf16),
+            pltpu.VMEM((model, ff), bf16),
+            pltpu.VMEM((ff, model), bf16),
+            pltpu.VMEM((N, rows, wd), bf16),
+            pltpu.VMEM((N, p, wd), bf16),
+            pltpu.VMEM((rows, cb), f32),
+            pltpu.VMEM((2 * STATE // cb, rows, cb), f32),
+            pltpu.VMEM((p, 128), f32),
+            pltpu.VMEM((N, p, 128), f32),
+            pltpu.VMEM((rows, wd), bf16),
+            pltpu.VMEM((N, rows, wd), bf16),
+            pltpu.VMEM((rows, ff), f32),
+            pltpu.VMEM((R, rows, wd), bf16),
+            pltpu.VMEM((R, rows, wd), bf16),
+            pltpu.VMEM((R, rows, wd), bf16),
+            pltpu.VMEM((R, rows, wd), bf16),
+            pltpu.VMEM((rows, wd), f32),
+            dma((6,)), dma((N,)), dma((N,)), dma((N,)), dma((N,)),
+            dma((N // GROUPS,)), dma((2 * STATE // cb,)),
+            dma((N,)), dma((N,)), dma((N,)), dma((N,)),
+            dma((R,)), dma((R,)), dma((R,)), dma((R,)),
+        ],
+        compiler_params=pltpu.CompilerParams(
+            collective_id=0, has_side_effects=True, vmem_limit_bytes=60 * 1024 * 1024
+        ),
+    )(
+        hidden,
+        norm_in_gain.reshape(1, model),
+        jnp.transpose(zx_weight, (1, 2, 3, 0)).reshape(2 * p, model),
+        bc_weight,
+        dt_weight.reshape(1, model),
+        dt_bias.reshape(1, 1),
+        decay_log.reshape(1, 1),
+        skip_gain.reshape(1, 1),
+        conv_x_weight.reshape(4, p),
+        conv_x_bias.reshape(1, p),
+        conv_bc_weight,
+        conv_bc_bias.reshape(1, cb),
+        jnp.transpose(conv_x_state, (1, 2, 0, 3)).reshape(3, rows, p),
+        jnp.transpose(conv_bc_state, (1, 0, 2)),
+        ssm_state.reshape(rows, p, STATE),
+        gate_norm_weight.reshape(1, p),
+        out_weight.reshape(p, model),
+        norm_mid_gain.reshape(1, model),
+        up_weight,
+        down_weight,
+        valid.reshape(1, rows),
+    )
+    return (
+        out,
+        new_ssm.reshape(rows, 1, p, STATE),
+        jnp.transpose(new_cx, (1, 0, 2)).reshape(rows, 3, 1, p),
+        jnp.transpose(new_cb, (1, 0, 2)),
+    )
+
+
 def solution(mesh):
+    chosen = fused_body if fits(mesh) else body
     return jax.shard_map(
-        body,
+        chosen,
         mesh=mesh,
         in_specs=(
             P("groups", ("row", "section")),

time: 252 us -> 73.2 us (0.29)
  waiting for transfers between devices: 107 us -> 0 us
  blocking collectives: 95 us -> 0 us
  Pallas kernels: 0 us -> 64.2 us
  matrix products: 23.5 us -> 0 us
  between operations: 16.2 us -> 2.58 us
  other arithmetic: 9.25 us -> 0 us
  local copies, waits for them, and re-layouts: 0.52 us -> 5.93 us
    reduce_scatter x2 -> x0, waiting for transfers between devices: 107 us -> none  [the longest x1 54.8 us: body(): lax.psum_scatter(mixer_terms, ('row', 'section'), scatter_dimension=1, ti...]
    pallas_call x0 -> x1, Pallas kernels: none -> 64.2 us  [fused_body(): pl.pallas_call(functools.partial(fused_kernel, R), out_shape=(jax.ShapeDt...]
    all_gather x3 -> x0, blocking collectives: 63.9 us -> none  [the longest x1 24.9 us: body(): full_rows = lax.all_gather(hidden, ('row', 'section'), axis=1, tiled=True)]
    psum x1 -> x0, blocking collectives: 31.1 us -> none  [body(): lax.psum(local_squares[:, None] * group_pick[None], ('row', 'section'))]
    dot_general x6 -> x0, matrix products: 23.5 us -> none  [the longest x1 14.8 us: body(): jnp.dot(activated, down_weight, preferred_element_type=jnp.float32)]
    unnamed x11 -> x4, local copies, waits for them, and re-layouts: 0.04 us -> 5.93 us
    convert_element_type x4 -> x0, other arithmetic: 3.5 us -> none  [the longest x1 1.46 us: body(): block_out = (middle.astype(jnp.float32) + down_share).astype(jnp.bfloat16)]
    reduce_sum x6 -> x0, other arithmetic: 2.85 us -> none  [the longest x1 0.77 us: body(): local_squares = jnp.sum(gated * gated, axis=(1, 2))]
  transfers between devices with their start and end apart: 2 -> 0, of which waited for: 2 -> 0; matrix products, arithmetic and copies ran while one was open for 1% -> 0% of each run, Pallas kernels for 0% -> 0%
where the time goes in v1:
time: 73.2 us; the launch traced here: 72.7 us
  Pallas kernels  64.2 us (88%)
  local copies, waits for them, and re-layouts  5.93 us (8%)
  between operations  2.58 us (4%)
    pallas_call x1, Pallas kernels, fused_body(): pl.pallas_call(functools.partial(fused_kernel, R), out_shape=(jax.ShapeDt...  64.2 us
    unnamed x4, local copies, waits for them, and re-layouts  5.93 us

profile of v1, /device:TPU:0, one launch (start us, length us, event | category | flops | bytes accessed | tf_op | source)
XLA Modules:
  0.0 72.7 jit_solution(342133840343358414)
XLA Ops:
  2.6 64.2 %shard_map.228 = (bf16[32,512]{1,0:T(8,128)(2,1)}, bf16[32,32,256]{2,1,0:T(8,128)(2,1)}, bf16[3,32,32]{2,1,0:T(8,128)(2,1)}, bf16[3,32,128]{2,1,0:T(8,128)(2,1)}) custom-call(bf16[32,512]{1,0:T(8,128)(2,1)} %hid.1, f32[1,8192]{1,0:T(1,128)} %bitcast.36, bf16[64,8192]{1,0:T(8,128)(2,1)} %bitcast.32, bf16[8192,128]{1,0:T(8,128)(2,1)} %bcw.1, ...), custom_call_target="tpu_custom_call" | custom-call | tf_op jit(solution)/shard_map/pallas_call | solution.py:449
  66.8 1.4 %copy.35 = bf16[32,512]{1,0:T(8,128)(2,1)} copy(bf16[32,512]{1,0:T(8,128)(2,1)} %get-tuple-element.20) | data formatting | bytes 65536
  68.1 1.9 %copy.36 = bf16[32,1,32,256]{3,2,1,0:T(8,128)(2,1)} copy(bf16[32,1,32,256]{3,2,1,0:T(8,128)(2,1)} %bitcast.35) | data formatting | bytes 1048576
  70.0 1.3 %copy.37 = bf16[32,3,1,32]{3,0,2,1:T(8,128)(2,1)} copy(bf16[32,3,1,32]{3,0,2,1:T(8,128)(2,1)} %bitcast.42) | data formatting | bytes 12288
  71.4 1.3 %copy.38 = bf16[32,3,128]{2,0,1:T(8,128)(2,1)} copy(bf16[32,3,128]{2,0,1:T(8,128)(2,1)} %bitcast.41) | data formatting | bytes 49152

commit v2 on v1

--- a/solution.py
+++ b/solution.py
@@ -115,9 +115,7 @@
 
 
 def fits(mesh):
-    rows, sections = mesh.shape["row"], mesh.shape["section"]
-    devices = rows * sections
-    return sections == 2 and devices == 16 and rows % GROUPS == 0
+    return mesh.shape["section"] == 2 and mesh.shape["row"] == 2 * GROUPS
 
 
 def silu(values):
@@ -130,9 +128,9 @@
     upw, dnw, valid,
     out, new_ssm, new_cx, new_cb,
     zx_v, bc_v, ssm_v, up_v, dn_v, hid_all, owt, bc_out, bc_all, g_out, g_all, mid, mid_all,
-    act, send_a, recv_a, send_b, recv_b, own_sum,
+    send_m, recv_m, act, send_a, recv_a, send_b, recv_b, own_sum,
     w_sem, h_send, h_recv, o_send, o_recv, bc_send, bc_recv, g_send, g_recv, m_send, m_recv,
-    a_send, a_recv, b_send, b_recv,
+    a_send, a_recv, b_send, b_recv, x_send, x_recv,
 ):
     N = 2 * R
     grp, row, sec = lax.axis_index("groups"), lax.axis_index("row"), lax.axis_index("section")
@@ -169,25 +167,44 @@
     hid_all[me] = hid[...]
     pl.semaphore_wait(barrier, N - 1)
 
+    Z = R // 2
+    z, x = row // 2, row % 2
+
     def gather_start(src, buf, ssem, rsem):
-        for k in range(1, R):
-            copy = remote(src, buf.at[me], ssem.at[k], rsem.at[me], lax.rem(row + k, R), sec)
-            copy.start()
-            pending.append(copy)
-        copy = remote(src, buf.at[me], ssem.at[0], rsem.at[me], row, other)
-        copy.start()
-        pending.append(copy)
-
-    def gather_finish(buf, ssem, rsem):
-        for k in range(1, R):
-            blk = lax.rem(row + R - k, R) * 2 + sec
-            copy = remote(buf.at[blk], buf.at[blk], ssem.at[R + k - 1], rsem.at[blk], row, other)
-            copy.wait_recv()
-            copy.start()
-            pending.append(copy)
-        for k in range(R):
-            blk = lax.rem(row + R - k, R) * 2 + other
-            remote(buf.at[blk], buf.at[blk], ssem.at[0], rsem.at[blk], row, other).wait_recv()
+        for k in range(1, Z):
+            remote(
+                src, buf.at[me], ssem.at[k], rsem.at[me], lax.rem(z + k, Z) * 2 + x, sec
+            ).start()
+        remote(src, buf.at[me], ssem.at[0], rsem.at[me], z * 2 + 1 - x, sec).start()
+        remote(src, buf.at[me], ssem.at[Z], rsem.at[me], row, other).start()
+
+    def gather_step(j, buf, ssem, rsem):
+        k, far, cross = j % Z, (j // Z) % 2, j // (2 * Z)
+        blk = (lax.rem(z + k, Z) * 2 + lax.rem(x + far, 2)) * 2 + lax.rem(sec + cross, 2)
+        block = buf.at[blk]
+
+        @pl.when(j > 0)
+        def _():
+            remote(block, block, ssem.at[0], rsem.at[blk], row, other).wait_recv()
+
+        @pl.when(jnp.logical_and(j > 0, j < Z))
+        def _():
+            remote(
+                block, block, ssem.at[Z + j], rsem.at[blk], z * 2 + 1 - x, sec
+            ).start()
+
+        @pl.when(jnp.logical_and(j > 0, j < 2 * Z))
+        def _():
+            remote(block, block, ssem.at[2 * Z + j - 1], rsem.at[blk], row, other).start()
+
+        return blk
+
+    def gather_drain(buf, ssem, rsem):
+        def step(i, _):
+            remote(buf.at[me], buf.at[me], ssem.at[i], rsem.at[me], row, other).wait_send()
+            return 0
+
+        lax.fori_loop(0, 4 * Z - 1, step, 0)
 
     gather_start(hid, hid_all, h_send, h_recv)
 
@@ -208,52 +225,45 @@
     gnw_t = turn(gnw[...])
     pre_bc = cbb[...] + sum(cbs[t].astype(f32) * cbw[t : t + 1, :] for t in range(3))
 
-    gather_finish(hid_all, h_send, h_recv)
-
-    for k in range(1, N):
-        peer = lax.rem(me + k, N)
-        copy = remote(
-            outw.at[:, pl.ds(pl.multiple_of(peer * wd, wd), wd)],
-            owt.at[me], o_send.at[k], o_recv.at[me], peer // 2, peer % 2,
-        )
-        copy.start()
-        pending.append(copy)
-    own_w = pltpu.make_async_copy(
-        outw.at[:, pl.ds(pl.multiple_of(me * wd, wd), wd)], owt.at[me], w_sem.at[5]
-    )
-    own_w.start()
-
-    def inverse_norm(buf):
-        def step(b, total):
-            values = buf[b].astype(f32)
-            squares = values * values
-            return total + sum(squares[:, i : i + 128] for i in range(0, wd, 128))
-
-        total = lax.fori_loop(0, N, step, jnp.zeros((rows, 128), f32))
+    def add_squares(total, values):
+        squares = values * values
+        return total + sum(squares[:, i : i + 128] for i in range(0, wd, 128))
+
+    def inverse(total):
         return lax.rsqrt(jnp.sum(total, axis=1, keepdims=True) / model + 1e-05)
 
-    scale = inverse_norm(hid_all)
     loads[0].wait()
     loads[1].wait()
 
-    def project(b, carry):
-        acc_bc, acc_zx, acc_dt = carry
+    def project(j, carry):
+        total, acc_bc, acc_zx, acc_dt = carry
+        b = gather_step(j, hid_all, h_send, h_recv)
         at = pl.ds(pl.multiple_of(b * wd, wd), wd)
-        normed = (hid_all[b].astype(f32) * scale * gin[:, at]).astype(jnp.bfloat16)
-        acc_bc += jnp.dot(normed, bc_v[at, :], preferred_element_type=f32)
-        acc_zx += lax.dot_general(zx_v[:, at], normed, NT, preferred_element_type=f32)
+        values = hid_all[b].astype(f32)
+        total = add_squares(total, values)
+        fed = (values * gin[:, at]).astype(jnp.bfloat16)
+        acc_bc += jnp.dot(fed, bc_v[at, :], preferred_element_type=f32)
+        acc_zx += lax.dot_general(zx_v[:, at], fed, NT, preferred_element_type=f32)
         dt_rows = jnp.broadcast_to(dtt[:, at].astype(f32), (16, wd)).astype(jnp.bfloat16)
-        acc_dt += lax.dot_general(dt_rows, normed, NT, preferred_element_type=f32)
-        return acc_bc, acc_zx, acc_dt
-
-    acc_bc, acc_zx, acc_dt = lax.fori_loop(
+        acc_dt += lax.dot_general(dt_rows, fed, NT, preferred_element_type=f32)
+        return total, acc_bc, acc_zx, acc_dt
+
+    total, acc_bc, acc_zx, acc_dt = lax.fori_loop(
         0, N, project,
         (
+            jnp.zeros((rows, 128), f32),
             jnp.zeros((rows, bc_v.shape[1]), f32),
             jnp.zeros((2 * local_p, rows), f32),
             jnp.zeros((16, rows), f32),
         ),
     )
+    scale = inverse(total)
+    eye_rows = (
+        lax.broadcasted_iota(jnp.int32, (rows, rows), 0)
+        == lax.broadcasted_iota(jnp.int32, (rows, rows), 1)
+    ).astype(f32)
+    scale_row = jnp.sum(eye_rows * scale, axis=0, keepdims=True)
+    acc_bc, acc_zx, acc_dt = acc_bc * scale, acc_zx * scale_row, acc_dt * scale_row
     bc_pre = acc_bc.astype(jnp.bfloat16).astype(f32)
     mixed_bc = silu(pre_bc + bc_pre * cbw[3:4, :])
     bc_out[...] = mixed_bc
@@ -277,6 +287,25 @@
         @pl.when(dest == me)
         def _():
             bc_all[slot] = bc_out[...]
+
+    place = x * 2 + sec
+    spots = [(1 - x, sec), (row % 2, other), (1 - x, other)]
+    for i, (px, pc) in enumerate(spots):
+        for t in range(Z):
+            at = pl.ds(pl.multiple_of((t * 4 + px * 2 + pc) * wd, wd), wd)
+            copy = remote(
+                outw.at[:, at], owt.at[t * 4 + place], o_send.at[i * Z + t],
+                o_recv.at[t * 4 + place], z * 2 + px, pc,
+            )
+            copy.start()
+            pending.append(copy)
+    own_w = []
+    for t in range(Z):
+        at = pl.ds(pl.multiple_of((t * 4 + place) * wd, wd), wd)
+        own_w.append(
+            pltpu.make_async_copy(outw.at[:, at], owt.at[t * 4 + place], w_sem.at[6 + t])
+        )
+        own_w[-1].start()
 
     gate_t = silu(acc_zx[:local_p])
     inner_pre_t = acc_zx[local_p:].astype(jnp.bfloat16).astype(f32)
@@ -324,53 +353,81 @@
     gated_t = (read_t + skip[...] * inner_t) * gate_t
     g_out[:, 0:rows] = gated_t
     g_out[:, rows : rows + 1] = gnw_t
-    gather_start(g_out, g_all, g_send, g_recv)
-    g_all[me] = g_out[...]
+    for i, (px, pc) in enumerate(spots):
+        copy = remote(
+            g_out, g_all.at[place], g_send.at[i], g_recv.at[place], z * 2 + px, pc
+        )
+        copy.start()
+        pending.append(copy)
+    g_all[place] = g_out[...]
 
     for r in range(rows):
         previous, value = updated(r)
         keep = jnp.broadcast_to(valid_row[0:1, r : r + 1], value.shape) > 0.5
-        new_ssm[r] = jnp.where(keep, value, previous).astype(jnp.bfloat16)
-
-    for k in range(1, N):
-        peer = lax.rem(me + N - k, N)
-        remote(owt.at[peer], owt.at[peer], o_send.at[0], o_recv.at[peer], row, other).wait_recv()
-    own_w.wait()
-    gather_finish(g_all, g_send, g_recv)
-
-    eye_rows = (
-        lax.broadcasted_iota(jnp.int32, (rows, rows), 0)
-        == lax.broadcasted_iota(jnp.int32, (rows, rows), 1)
+        ssm_v[r] = jnp.where(keep, value, previous).astype(jnp.bfloat16)
+    store_ssm = pltpu.make_async_copy(ssm_v, new_ssm, w_sem.at[5])
+    store_ssm.start()
+
+    for copy in own_w:
+        copy.wait()
+    for px, pc in spots:
+        there = px * 2 + pc
+        for t in range(Z):
+            spot = t * 4 + there
+            remote(
+                owt.at[spot], owt.at[spot], o_send.at[0], o_recv.at[spot], row, other
+            ).wait_recv()
+    for px, pc in spots:
+        there = px * 2 + pc
+        remote(
+            g_all.at[there], g_all.at[there], g_send.at[0], g_recv.at[there], row, other
+        ).wait_recv()
+
+    pieces = [g_all[i, :, 0:rows] for i in range(4)]
+    squares = sum(jnp.sum(piece * piece, axis=0, keepdims=True) for piece in pieces)
+    norm = lax.rsqrt(squares / (4 * local_p) + 1e-05)
+    scaled_t = jnp.concatenate(
+        [pieces[i] * norm * g_all[i, :, rows : rows + 1] for i in range(4)], axis=0
     ).astype(jnp.bfloat16)
-    mixed = hid[...].astype(f32)
-    for q in range(GROUPS):
-        pieces = [g_all[q * per + i, :, 0:rows] for i in range(per)]
-        squares = sum(jnp.sum(piece * piece, axis=0, keepdims=True) for piece in pieces)
-        norm = lax.rsqrt(squares / (per * local_p) + 1e-05)
-        scaled_t = jnp.concatenate(
-            [pieces[i] * norm * g_all[q * per + i, :, rows : rows + 1] for i in range(per)], axis=0
-        ).astype(jnp.bfloat16)
-        scaled = lax.dot_general(eye_rows, scaled_t, NT, preferred_element_type=f32)
-        weights = owt[q * per : (q + 1) * per].reshape(per * local_p, wd)
-        mixed += jnp.dot(scaled.astype(jnp.bfloat16), weights, preferred_element_type=f32)
+    scaled = lax.dot_general(
+        eye_rows.astype(jnp.bfloat16), scaled_t, NT, preferred_element_type=f32
+    ).astype(jnp.bfloat16)
+
+    def mixer(t):
+        weights = owt[pl.ds(t * 4, 4)].reshape(4 * local_p, wd)
+        return jnp.dot(scaled, weights, preferred_element_type=f32)
+
+    for k in (2, 1, 3):
+        t = lax.rem(z + k, Z)
+        send_m[k] = mixer(t).astype(jnp.bfloat16)
+        copy = remote(
+            send_m.at[k], recv_m.at[z], x_send.at[k], x_recv.at[z], t * 2 + x, sec
+        )
+        copy.start()
+        pending.append(copy)
+    mixed = hid[...].astype(f32) + mixer(z)
+    for k in (1, 3, 2):
+        t = lax.rem(z + k, Z)
+        remote(
+            recv_m.at[t], recv_m.at[t], x_send.at[0], x_recv.at[t], row, other
+        ).wait_recv()
+        mixed += recv_m[t].astype(f32)
     mid[...] = mixed.astype(jnp.bfloat16)
     gather_start(mid, mid_all, m_send, m_recv)
     mid_all[me] = mid[...]
-    gather_finish(mid_all, m_send, m_recv)
-
-    scale_mid = inverse_norm(mid_all)
     loads[3].wait()
-    ff = up_v.shape[1]
     act[...] = jnp.zeros_like(act)
 
-    def up_step(b, _):
+    def up_step(j, total):
+        b = gather_step(j, mid_all, m_send, m_recv)
         at = pl.ds(pl.multiple_of(b * wd, wd), wd)
-        fed = (mid_all[b].astype(f32) * scale_mid * gmid[:, at]).astype(jnp.bfloat16)
+        values = mid_all[b].astype(f32)
+        fed = (values * gmid[:, at]).astype(jnp.bfloat16)
         act[...] += jnp.dot(fed, up_v[at, :], preferred_element_type=f32)
-        return 0
-
-    lax.fori_loop(0, N, up_step, 0)
-    activated = jnp.square(jnp.maximum(act[...], 0.0)).astype(jnp.bfloat16)
+        return add_squares(total, values)
+
+    total = lax.fori_loop(0, N, up_step, jnp.zeros((rows, 128), f32))
+    activated = jnp.square(jnp.maximum(act[...] * inverse(total), 0.0)).astype(jnp.bfloat16)
     loads[4].wait()
 
     def down(block):
@@ -429,6 +486,35 @@
 
     for copy in pending:
         copy.wait_send()
+    gather_drain(hid_all, h_send, h_recv)
+    gather_drain(mid_all, m_send, m_recv)
+    store_ssm.wait()
+
+
+def hand_over(*refs):
+    count = (len(refs) - 2) // 3
+    ins, outs, held = refs[:count], refs[count : 2 * count], refs[2 * count : 3 * count]
+    in_sem, out_sem = refs[3 * count], refs[3 * count + 1]
+    parts = []
+    for i in range(count):
+        cuts = 4 if i == 1 else 1
+        size = ins[i].shape[0] // cuts
+        for c in range(cuts):
+            at = pl.ds(c * size, size)
+            n = len(parts)
+            parts.append(
+                (
+                    pltpu.make_async_copy(ins[i].at[at], held[i].at[at], in_sem.at[n]),
+                    pltpu.make_async_copy(held[i].at[at], outs[i].at[at], out_sem.at[n]),
+                )
+            )
+    for first, _ in parts:
+        first.start()
+    for first, second in parts:
+        first.wait()
+        second.start()
+    for _, second in parts:
+        second.wait()
 
 
 def fused_body(
@@ -446,7 +532,7 @@
     bf16, f32 = jnp.bfloat16, jnp.float32
     vm, hbm = pl.BlockSpec(memory_space=pltpu.VMEM), pl.BlockSpec(memory_space=pl.ANY)
     dma = pltpu.SemaphoreType.DMA
-    out, new_ssm, new_cx, new_cb = pl.pallas_call(
+    results = pl.pallas_call(
         functools.partial(fused_kernel, R),
         out_shape=(
             jax.ShapeDtypeStruct((rows, wd), bf16),
@@ -457,7 +543,7 @@
         in_specs=[
             vm, vm, hbm, hbm, vm, vm, vm, vm, vm, vm, vm, vm, vm, vm, hbm, vm, hbm, vm, hbm, hbm, vm
         ],
-        out_specs=(vm, vm, vm, vm),
+        out_specs=(vm, hbm, vm, vm),
         scratch_shapes=[
             pltpu.VMEM((2 * p, model), bf16),
             pltpu.VMEM((model, cb), bf16),
@@ -469,19 +555,21 @@
             pltpu.VMEM((rows, cb), f32),
             pltpu.VMEM((2 * STATE // cb, rows, cb), f32),
             pltpu.VMEM((p, 128), f32),
-            pltpu.VMEM((N, p, 128), f32),
+            pltpu.VMEM((4, p, 128), f32),
             pltpu.VMEM((rows, wd), bf16),
             pltpu.VMEM((N, rows, wd), bf16),
+            pltpu.VMEM((R // 2, rows, wd), bf16),
+            pltpu.VMEM((R // 2, rows, wd), bf16),
             pltpu.VMEM((rows, ff), f32),
             pltpu.VMEM((R, rows, wd), bf16),
             pltpu.VMEM((R, rows, wd), bf16),
             pltpu.VMEM((R, rows, wd), bf16),
             pltpu.VMEM((R, rows, wd), bf16),
             pltpu.VMEM((rows, wd), f32),
-            dma((6,)), dma((N,)), dma((N,)), dma((N,)), dma((N,)),
+            dma((6 + R // 2,)), dma((N,)), dma((N,)), dma((N,)), dma((N,)),
             dma((N // GROUPS,)), dma((2 * STATE // cb,)),
             dma((N,)), dma((N,)), dma((N,)), dma((N,)),
-            dma((R,)), dma((R,)), dma((R,)), dma((R,)),
+            dma((R,)), dma((R,)), dma((R,)), dma((R,)), dma((R,)), dma((R,)),
         ],
         compiler_params=pltpu.CompilerParams(
             collective_id=0, has_side_effects=True, vmem_limit_bytes=60 * 1024 * 1024
@@ -509,6 +597,13 @@
         down_weight,
         valid.reshape(1, rows),
     )
+    out, new_ssm, new_cx, new_cb = pl.pallas_call(
+        hand_over,
+        out_shape=tuple(jax.ShapeDtypeStruct(v.shape, v.dtype) for v in results),
+        in_specs=[hbm] * 4,
+        out_specs=(hbm,) * 4,
+        scratch_shapes=[pltpu.VMEM(v.shape, v.dtype) for v in results] + [dma((7,)), dma((7,))],
+    )(*results)
     return (
         out,
         new_ssm.reshape(rows, 1, p, STATE),

time: 73.2 us -> 58.2 us (0.80)
  Pallas kernels: 64.2 us -> 55.3 us
  local copies, waits for them, and re-layouts: 5.93 us -> 0 us
    pallas_call x1, Pallas kernels: 64.2 us -> 53.4 us  [fused_body(): pl.pallas_call(functools.partial(fused_kernel, R), out_shape=(jax.ShapeDt...]
    unnamed x4 -> x0, local copies, waits for them, and re-layouts: 5.93 us -> none
    pallas_call x0 -> x1, Pallas kernels: none -> 1.9 us  [fused_body(): pl.pallas_call(hand_over, out_shape=tuple((jax.ShapeDtypeStruct(v.shape,...]
where the time goes in v2:
time: 58.2 us; the launch traced here: 57.9 us
  Pallas kernels  55.3 us (95%)
  between operations  2.58 us (4%)
    pallas_call x1, Pallas kernels, fused_body(): pl.pallas_call(functools.partial(fused_kernel, R), out_shape=(jax.ShapeDt...  53.4 us
    pallas_call x1, Pallas kernels, fused_body(): pl.pallas_call(hand_over, out_shape=tuple((jax.ShapeDtypeStruct(v.shape,...  1.9 us

profile of v2, /device:TPU:0, one launch (start us, length us, event | category | flops | bytes accessed | tf_op | source)
XLA Modules:
  0.0 57.9 jit_solution(17075462867601104323)
XLA Ops:
  2.6 53.4 %shard_map.228 = (bf16[32,512]{1,0:T(8,128)(2,1)}, bf16[32,32,256]{2,1,0:T(8,128)(2,1)}, bf16[3,32,32]{2,1,0:T(8,128)(2,1)}, bf16[3,32,128]{2,1,0:T(8,128)(2,1)}) custom-call(bf16[32,512]{1,0:T(8,128)(2,1)} %hid.1, f32[1,8192]{1,0:T(1,128)} %bitcast.35, bf16[64,8192]{1,0:T(8,128)(2,1)} %bitcast.32, bf16[8192,128]{1,0:T(8,128)(2,1)} %bcw.1, ...), custom_call_target="tpu_custom_call" | custom-call | tf_op jit(solution)/shard_map/pallas_call | solution.py:535
  56.0 1.9 %shard_map.229 = (bf16[32,512]{1,0:T(8,128)(2,1)}, bf16[32,32,256]{2,1,0:T(8,128)(2,1)}, bf16[3,32,32]{2,1,0:T(8,128)(2,1)}, bf16[3,32,128]{2,1,0:T(8,128)(2,1)}) custom-call(bf16[32,512]{1,0:T(8,128)(2,1)} %get-tuple-element.12.refs_0_, bf16[32,32,256]{2,1,0:T(8,128)(2,1)} %get-tuple-element.13.refs_1_, bf16[3,32,32]{2,1,0:T(8,128)(2,1)} %get-tuple-element.14.refs_2_, ...), custom_call_target="tpu_custom_call" | custom-call | tf_op jit(solution)/shard_map/pallas_call | solution.py:600

commit v3 on v2

--- a/solution.py
+++ b/solution.py
@@ -122,8 +122,21 @@
     return values / (1.0 + jnp.exp(-values))
 
 
+SMALL = (0, 1, 4, 5, 6, 7, 8, 9, 10, 11, 12, 13, 15, 17, 20)
+
+
+def staged_kernel(R, *refs):
+    count = len(SMALL)
+    ins, rest, held, sem = list(refs[:21]), refs[21 : -count - 1], refs[-count - 1 : -1], refs[-1]
+    copies = [pltpu.make_async_copy(ins[i], held[n], sem.at[n]) for n, i in enumerate(SMALL)]
+    hid_source = ins[0]
+    for n, i in enumerate(SMALL):
+        ins[i] = held[n]
+    fused_kernel(R, copies, hid_source, *ins, *rest)
+
+
 def fused_kernel(
-    R,
+    R, small_copies, hid_source,
     hid, gin, zxt, bcw, dtt, dtb, dlog, skip, cxw, cxb, cbw, cbb, cxs, cbs, ssm, gnw, outw, gmid,
     upw, dnw, valid,
     out, new_ssm, new_cx, new_cb,
@@ -162,9 +175,8 @@
         pl.semaphore_signal(
             barrier, inc=1, device_id=(grp, peer // 2, peer % 2), device_id_type=MESH
         )
-    for copy in loads:
+    for copy in small_copies + loads:
         copy.start()
-    hid_all[me] = hid[...]
     pl.semaphore_wait(barrier, N - 1)
 
     Z = R // 2
@@ -178,7 +190,12 @@
         remote(src, buf.at[me], ssem.at[0], rsem.at[me], z * 2 + 1 - x, sec).start()
         remote(src, buf.at[me], ssem.at[Z], rsem.at[me], row, other).start()
 
-    def gather_step(j, buf, ssem, rsem):
+    visits = (0, 8, 4, 1, 3, 12, 5, 7, 2, 9, 11, 6, 13, 15, 10, 14)
+
+    def gather_step(i, buf, ssem, rsem):
+        j = jnp.int32(0)
+        for position, visit in enumerate(visits):
+            j = jnp.where(i == position, visit, j)
         k, far, cross = j % Z, (j // Z) % 2, j // (2 * Z)
         blk = (lax.rem(z + k, Z) * 2 + lax.rem(x + far, 2)) * 2 + lax.rem(sec + cross, 2)
         block = buf.at[blk]
@@ -206,7 +223,10 @@
 
         lax.fori_loop(0, 4 * Z - 1, step, 0)
 
-    gather_start(hid, hid_all, h_send, h_recv)
+    gather_start(hid_source, hid_all, h_send, h_recv)
+    for copy in small_copies:
+        copy.wait()
+    hid_all[me] = hid[...]
 
     eye = (
         lax.broadcasted_iota(jnp.int32, (local_p, local_p), 0)
@@ -434,23 +454,37 @@
         at = pl.ds(pl.multiple_of(block * wd, wd), wd)
         return jnp.dot(activated, dn_v[:, at], preferred_element_type=f32)
 
-    def for_partner(k, _):
-        target = lax.rem(row + 1 + k, R)
-        send_a[k] = down(target * 2 + other).astype(jnp.bfloat16)
+    def target_of(k):
+        hop = jnp.where(k < 2, 2, jnp.where(k < 4, 1, jnp.where(k < 6, 3, 0)))
+        return lax.rem(z + hop, Z) * 2 + lax.rem(x + 1 + k, 2)
+
+    def for_partner(k):
+        send_a[k] = down(target_of(k) * 2 + other).astype(jnp.bfloat16)
         remote(send_a.at[k], recv_a.at[k], a_send.at[k], a_recv.at[k], row, other).start()
-        return 0
-
-    lax.fori_loop(0, R, for_partner, 0)
-
-    def for_chip(k, _):
-        target = lax.rem(row + 1 + k, R)
+
+    def for_chip(k):
+        target = target_of(k)
         part = down(target * 2 + sec)
         remote(send_a.at[k], recv_a.at[k], a_send.at[k], a_recv.at[k], row, other).wait()
         send_b[k] = (part + recv_a[k].astype(f32)).astype(jnp.bfloat16)
         remote(send_b.at[k], recv_b.at[row], b_send.at[k], b_recv.at[row], target, sec).start()
+
+    def first_step(k, _):
+        for_partner(k)
         return 0
 
-    lax.fori_loop(0, R - 1, for_chip, 0)
+    def both_step(k, _):
+        for_partner(k + 2)
+        for_chip(k)
+        return 0
+
+    def last_step(k, _):
+        for_chip(k)
+        return 0
+
+    lax.fori_loop(0, 2, first_step, 0)
+    lax.fori_loop(0, R - 2, both_step, 0)
+    lax.fori_loop(R - 2, R - 1, last_step, 0)
     total = down(me)
     remote(
         send_a.at[R - 1], recv_a.at[R - 1], a_send.at[R - 1], a_recv.at[R - 1], row, other
@@ -458,7 +492,7 @@
     own_sum[...] = total + recv_a[R - 1].astype(f32) + mid[...].astype(f32)
 
     def collect(k, _):
-        source = lax.rem(row + R - 1 - k, R)
+        source = target_of(lax.rem(k + R - 2, R - 1))
         remote(
             send_b.at[k], recv_b.at[source], b_send.at[k], b_recv.at[source], source, sec
         ).wait_recv()
@@ -532,17 +566,38 @@
     bf16, f32 = jnp.bfloat16, jnp.float32
     vm, hbm = pl.BlockSpec(memory_space=pltpu.VMEM), pl.BlockSpec(memory_space=pl.ANY)
     dma = pltpu.SemaphoreType.DMA
+    operands = (
+        hidden,
+        norm_in_gain.reshape(1, model),
+        jnp.transpose(zx_weight, (1, 2, 3, 0)).reshape(2 * p, model),
+        bc_weight,
+        dt_weight.reshape(1, model),
+        dt_bias.reshape(1, 1),
+        decay_log.reshape(1, 1),
+        skip_gain.reshape(1, 1),
+        conv_x_weight.reshape(4, p),
+        conv_x_bias.reshape(1, p),
+        conv_bc_weight,
+        conv_bc_bias.reshape(1, cb),
+        jnp.transpose(conv_x_state, (1, 2, 0, 3)).reshape(3, rows, p),
+        jnp.transpose(conv_bc_state, (1, 0, 2)),
+        ssm_state.reshape(rows, p, STATE),
+        gate_norm_weight.reshape(1, p),
+        out_weight.reshape(p, model),
+        norm_mid_gain.reshape(1, model),
+        up_weight,
+        down_weight,
+        valid.reshape(1, rows),
+    )
     results = pl.pallas_call(
-        functools.partial(fused_kernel, R),
+        functools.partial(staged_kernel, R),
         out_shape=(
             jax.ShapeDtypeStruct((rows, wd), bf16),
             jax.ShapeDtypeStruct((rows, p, STATE), bf16),
             jax.ShapeDtypeStruct((3, rows, p), bf16),
             jax.ShapeDtypeStruct((3, rows, cb), bf16),
         ),
-        in_specs=[
-            vm, vm, hbm, hbm, vm, vm, vm, vm, vm, vm, vm, vm, vm, vm, hbm, vm, hbm, vm, hbm, hbm, vm
-        ],
+        in_specs=[hbm] * 21,
         out_specs=(vm, hbm, vm, vm),
         scratch_shapes=[
             pltpu.VMEM((2 * p, model), bf16),
@@ -570,33 +625,13 @@
             dma((N // GROUPS,)), dma((2 * STATE // cb,)),
             dma((N,)), dma((N,)), dma((N,)), dma((N,)),
             dma((R,)), dma((R,)), dma((R,)), dma((R,)), dma((R,)), dma((R,)),
-        ],
+        ]
+        + [pltpu.VMEM(operands[i].shape, operands[i].dtype) for i in SMALL]
+        + [dma((len(SMALL),))],
         compiler_params=pltpu.CompilerParams(
             collective_id=0, has_side_effects=True, vmem_limit_bytes=60 * 1024 * 1024
         ),
-    )(
-        hidden,
-        norm_in_gain.reshape(1, model),
-        jnp.transpose(zx_weight, (1, 2, 3, 0)).reshape(2 * p, model),
-        bc_weight,
-        dt_weight.reshape(1, model),
-        dt_bias.reshape(1, 1),
-        decay_log.reshape(1, 1),
-        skip_gain.reshape(1, 1),
-        conv_x_weight.reshape(4, p),
-        conv_x_bias.reshape(1, p),
-        conv_bc_weight,
-        conv_bc_bias.reshape(1, cb),
-        jnp.transpose(conv_x_state, (1, 2, 0, 3)).reshape(3, rows, p),
-        jnp.transpose(conv_bc_state, (1, 0, 2)),
-        ssm_state.reshape(rows, p, STATE),
-        gate_norm_weight.reshape(1, p),
-        out_weight.reshape(p, model),
-        norm_mid_gain.reshape(1, model),
-        up_weight,
-        down_weight,
-        valid.reshape(1, rows),
-    )
+    )(*operands)
     out, new_ssm, new_cx, new_cb = pl.pallas_call(
         hand_over,
         out_shape=tuple(jax.ShapeDtypeStruct(v.shape, v.dtype) for v in results),

time: 58.2 us -> 61.9 us (1.064)
  Pallas kernels: 55.3 us -> 59.1 us
    pallas_call x1, Pallas kernels: 53.4 us -> 57.2 us  [fused_body(): pl.pallas_call(functools.partial(staged_kernel, R), out_shape=(jax.ShapeD...]
where the time goes in v3:
time: 61.9 us; the launch traced here: 61.7 us
  Pallas kernels  59.1 us (95%)
  between operations  2.58 us (4%)
    pallas_call x1, Pallas kernels, fused_body(): pl.pallas_call(functools.partial(staged_kernel, R), out_shape=(jax.ShapeD...  57.2 us
    pallas_call x1, Pallas kernels, fused_body(): pl.pallas_call(hand_over, out_shape=tuple((jax.ShapeDtypeStruct(v.shape,...  1.9 us

profile of v3, /device:TPU:0, one launch (start us, length us, event | category | flops | bytes accessed | tf_op | source)
XLA Modules:
  0.0 61.7 jit_solution(15904837055661979802)
XLA Ops:
  2.6 57.2 %shard_map.228 = (bf16[32,512]{1,0:T(8,128)(2,1)}, bf16[32,32,256]{2,1,0:T(8,128)(2,1)}, bf16[3,32,32]{2,1,0:T(8,128)(2,1)}, bf16[3,32,128]{2,1,0:T(8,128)(2,1)}) custom-call(bf16[32,512]{1,0:T(8,128)(2,1)} %refs_0_.1, f32[1,8192]{1,0:T(1,128)} %bitcast.35, bf16[64,8192]{1,0:T(8,128)(2,1)} %bitcast.32, bf16[8192,128]{1,0:T(8,128)(2,1)} %refs_3_.1, ...), custom_call_target="tpu_custom_call" | custom-call | tf_op jit(solution)/shard_map/pallas_call | solution.py:592
  59.8 1.9 %shard_map.229 = (bf16[32,512]{1,0:T(8,128)(2,1)}, bf16[32,32,256]{2,1,0:T(8,128)(2,1)}, bf16[3,32,32]{2,1,0:T(8,128)(2,1)}, bf16[3,32,128]{2,1,0:T(8,128)(2,1)}) custom-call(bf16[32,512]{1,0:T(8,128)(2,1)} %get-tuple-element.12.refs_0_, bf16[32,32,256]{2,1,0:T(8,128)(2,1)} %get-tuple-element.13.refs_1_, bf16[3,32,32]{2,1,0:T(8,128)(2,1)} %get-tuple-element.14.refs_2_, ...), custom_call_target="tpu_custom_call" | custom-call | tf_op jit(solution)/shard_map/pallas_call | solution.py:635

commit v4 on v3

--- a/solution.py
+++ b/solution.py
@@ -190,7 +190,7 @@
         remote(src, buf.at[me], ssem.at[0], rsem.at[me], z * 2 + 1 - x, sec).start()
         remote(src, buf.at[me], ssem.at[Z], rsem.at[me], row, other).start()
 
-    visits = (0, 8, 4, 1, 3, 12, 5, 7, 2, 9, 11, 6, 13, 15, 10, 14)
+    visits = tuple(range(16))
 
     def gather_step(i, buf, ssem, rsem):
         j = jnp.int32(0)

time: 61.9 us -> 57.9 us (0.935)
  Pallas kernels: 59.1 us -> 55.2 us
    pallas_call x1, Pallas kernels: 57.2 us -> 53.3 us  [fused_body(): pl.pallas_call(functools.partial(staged_kernel, R), out_shape=(jax.ShapeD...]
where the time goes in v4:
time: 57.9 us; the launch traced here: 57.8 us
  Pallas kernels  55.2 us (95%)
  between operations  2.58 us (4%)
    pallas_call x1, Pallas kernels, fused_body(): pl.pallas_call(functools.partial(staged_kernel, R), out_shape=(jax.ShapeD...  53.3 us
    pallas_call x1, Pallas kernels, fused_body(): pl.pallas_call(hand_over, out_shape=tuple((jax.ShapeDtypeStruct(v.shape,...  1.9 us

profile of v4, /device:TPU:0, one launch (start us, length us, event | category | flops | bytes accessed | tf_op | source)
XLA Modules:
  0.0 57.8 jit_solution(5269551605511957349)
XLA Ops:
  2.6 53.3 %shard_map.228 = (bf16[32,512]{1,0:T(8,128)(2,1)}, bf16[32,32,256]{2,1,0:T(8,128)(2,1)}, bf16[3,32,32]{2,1,0:T(8,128)(2,1)}, bf16[3,32,128]{2,1,0:T(8,128)(2,1)}) custom-call(bf16[32,512]{1,0:T(8,128)(2,1)} %refs_0_.1, f32[1,8192]{1,0:T(1,128)} %bitcast.35, bf16[64,8192]{1,0:T(8,128)(2,1)} %bitcast.32, bf16[8192,128]{1,0:T(8,128)(2,1)} %refs_3_.1, ...), custom_call_target="tpu_custom_call" | custom-call | tf_op jit(solution)/shard_map/pallas_call | solution.py:592
  55.9 1.9 %shard_map.229 = (bf16[32,512]{1,0:T(8,128)(2,1)}, bf16[32,32,256]{2,1,0:T(8,128)(2,1)}, bf16[3,32,32]{2,1,0:T(8,128)(2,1)}, bf16[3,32,128]{2,1,0:T(8,128)(2,1)}) custom-call(bf16[32,512]{1,0:T(8,128)(2,1)} %get-tuple-element.12.refs_0_, bf16[32,32,256]{2,1,0:T(8,128)(2,1)} %get-tuple-element.13.refs_1_, bf16[3,32,32]{2,1,0:T(8,128)(2,1)} %get-tuple-element.14.refs_2_, ...), custom_call_target="tpu_custom_call" | custom-call | tf_op jit(solution)/shard_map/pallas_call | solution.py:635
